TPU v7x, 32 devices: a whole 2x2x4 slice. The times are simulated.
32 devices in a mesh: gx: 4 (over y, core), yz: 8 (over z, x).
Axes of the slice: x: 2, y: 2, z: 4, core: 2. Of those that a mesh axis runs over, the one named last changes fastest.
Arguments:
- flow_speed_field: float32 [3, 32, 64, 128], P(None, 'gx', 'yz'), may hold values from -6 to 6
- thermal_field: float32 [32, 64, 128], P('gx', 'yz'), may hold values from 0.5 to 2
- walker_speed_vectors: float32 [3, 4096, 128], P(None, ('gx', 'yz')), may hold values from -6 to 6
- walker_statistical_mass: float32 [4096, 128], P(('gx', 'yz')), may hold values from 0.5 to 2
- gaussian_samples: float32 [2, 3, 4096, 128], P(None, None, ('gx', 'yz')), may hold values from -6 to 6
- walker_strip_position: int32 [4096, 128], P(('gx', 'yz')), may hold values from 0 to 127
- group_active_tally: int32 [4096], P(('gx', 'yz')), may hold values from 32 to 128
- group_resident_strip: int32 [4096], P(('gx', 'yz')), may hold values from 0 to 63
- migrating_group_table: int32 [512], P(('gx', 'yz')), may hold values from 0 to 127, as said below
- target_processor_slot: int32 [512, 1], P(('gx', 'yz')), may hold values from 0 to 7; in each aligned block of 16 rows (0 to 15, 16 to 31, ...) at most 4 rows name the same one
- entered_strip_slot: int32 [512], P(('gx', 'yz')), may hold values from 0 to 63
Outputs:
- new_fields: float32 [4, 32, 64, 128], P(None, 'gx', 'yz')
- particle_velocity: float32 [3, 4096, 128], P(None, ('gx', 'yz'))
Inputs may be any that keep to these rules, and one draw needn't show every extreme that they name: `migrating_group_table`: within each device's 16 entries the block indices are distinct. `target_processor_slot`: among the 16 rows of one device no yz index appears more than 4 times.
All inputs are finite; a program needn't handle non-finite values.
Results may differ from a plain program's by a relative error of at most 0.00005.
Values sent between devices are 32-bit elements; how exact they have to be, the bound alone decides.
A program may use at most 64 MiB of HBM per device.

v0:
```python
import functools
import math

import jax
import jax.numpy as jnp
from jax import lax
from jax.experimental import pallas as pl
from jax.experimental.pallas import tpu as pltpu
from jax.sharding import PartitionSpec as P

DECAY = 0.6
VISCOSITY = 0.05
COUPLING = 0.02
STRESS_GAIN = 0.005
RELAXATION = 0.5
PAIRS = ((0, 0), (0, 1), (0, 2), (1, 1), (1, 2), (2, 2))
PAIR_INDEX = ((0, 1, 2), (1, 3, 4), (2, 4, 5))
MOMENTS = 10
PITCH = 16
SENT = 9
UNROLL = 32
LOAD_ORDER = (6, 7, 8, 9, 10, 0, 1, 5, 2, 3, 4)
MESH = pl.DeviceIdType.MESH
BF16 = jnp.bfloat16
F32 = jnp.float32


def split3(x):
    high = x.astype(BF16)
    rest = x - high.astype(F32)
    mid = rest.astype(BF16)
    low = (rest - mid.astype(F32)).astype(BF16)
    return high, mid, low


def dot(a, b):
    return jnp.dot(a, b, preferred_element_type=F32)


def dot_last(a, b):
    return lax.dot_general(a, b, (((1,), (1,)), ((), ())), preferred_element_type=F32)


def pick(onehot, x):
    high, mid, low = split3(x)
    return dot(onehot, high) + dot(onehot, mid) + dot(onehot, low)


def lanes(x, index):
    return jnp.take_along_axis(x, index, axis=1, mode="promise_in_bounds")


def onehot(condition):
    return jnp.where(condition, 1.0, 0.0)


def drift(start, u, spread, noise):
    return u + DECAY * (start - u) + spread * noise


def deposit(count, unroll, v_ref, cells_ref, pb_ref):
    width = v_ref.shape[1]
    slots = cells_ref.shape[1]
    where = lax.broadcasted_iota(jnp.int32, (width, slots), 0)

    def some(step, carry):
        for t in range(unroll):
            n = step * unroll + t
            row = pl.ds(pl.multiple_of(n * PITCH, PITCH), PITCH)
            lhs = jnp.concatenate(split3(v_ref[row, :]), axis=0)
            hot = onehot(cells_ref[pl.ds(n, 1), :] == where).astype(BF16)
            out = dot_last(lhs, hot)
            pb_ref[row, :] = out[:PITCH] + out[PITCH : 2 * PITCH] + out[2 * PITCH :]
        return carry

    lax.fori_loop(0, count // unroll, some, 0)


def put_terms(v_ref, count, weight, second):
    terms = (
        [weight]
        + [weight * second[row] for row in range(3)]
        + [weight * second[one] * second[two] for one, two in PAIRS]
    )
    for k, term in enumerate(terms):
        v_ref[pl.ds(k, count, stride=PITCH), :] = term


def kernel(
    n,
    n_gx,
    spans,
    *refs,
):
    sources, (fields_out, speed_out), held, load_s = refs[:11], refs[11:13], refs[13:24], refs[24]
    flow, heat, speed, mass, noise, cells, tally, home, table, target, entered = held
    (
    v_ref,
    pb_ref,
    second_ref,
    cells_a,
    moments,
    wide,
    face_send,
    face_recv,
    stress_send,
    stress_recv,
    out_ref,
    in_ref,
    back_send,
    back_recv,
    out_s,
    out_r,
    face_s,
    face_r,
    stress_s,
    stress_r,
    back_s,
    back_r,
    ) = refs[25:]
    loads = [
        pltpu.make_async_copy(source, kept, load_s.at[i])
        for i, (source, kept) in enumerate(zip(sources, held))
    ]
    X, Y, Z = spans
    pencils = X * Y
    blocks, slots = mass.shape
    moving = table.shape[1]
    cap = 2 * moving // n
    received = n * cap
    rows = out_ref.shape[0] // n
    back_rows = back_send.shape[0] // n
    gx = lax.axis_index("gx")
    me = lax.axis_index("yz")
    order = sorted(range(1, n), key=lambda i: abs(2 * i - n))
    peers = [(i, lax.rem(me + i, n), lax.rem(me + n - i, n)) for i in order]
    for i in LOAD_ORDER:
        loads[i].start()

    barrier = pltpu.get_barrier_semaphore()
    for _, peer, _ in peers:
        pl.semaphore_signal(barrier, inc=1, device_id={"yz": peer}, device_id_type=MESH)

    @pl.when(gx > 0)
    def _():
        pl.semaphore_signal(barrier, inc=1, device_id={"gx": gx - 1}, device_id_type=MESH)

    @pl.when(gx < n_gx - 1)
    def _():
        pl.semaphore_signal(barrier, inc=1, device_id={"gx": gx + 1}, device_id_type=MESH)

    sides = (
        (0, 1, gx > 0, gx == 0, {"gx": gx - 1}),
        (1, 0, gx < n_gx - 1, gx == n_gx - 1, {"gx": gx + 1}),
        (2, 3, me > 0, me == 0, {"yz": me - 1}),
        (3, 2, me < n - 1, me == n - 1, {"yz": me + 1}),
    )
    for side, _, _, edge, _ in sides:

        @pl.when(edge)
        def _(side=side):
            face_recv[side] = jnp.zeros(face_recv.shape[1:], F32)
            stress_recv[side] = jnp.zeros(stress_recv.shape[1:], F32)

    def face_copy(side, other, where, send, recv, send_sem, recv_sem):
        return pltpu.make_async_remote_copy(
            src_ref=send.at[side],
            dst_ref=recv.at[other],
            send_sem=send_sem.at[side],
            recv_sem=recv_sem.at[other],
            device_id=where,
            device_id_type=MESH,
        )

    def faces_start(send, recv, send_sem, recv_sem):
        for side, other, there, _, where in sides:

            @pl.when(there)
            def _(side=side, other=other, where=where):
                face_copy(side, other, where, send, recv, send_sem, recv_sem).start()

    def faces_wait(send, recv, send_sem, recv_sem):
        for side, _, there, _, where in sides:

            @pl.when(there)
            def _(side=side, where=where):
                face_copy(side, side, where, send, recv, send_sem, recv_sem).wait_recv()

    def faces_sent(send, recv, send_sem, recv_sem):
        for side, other, there, _, where in sides:

            @pl.when(there)
            def _(side=side, other=other, where=where):
                face_copy(side, other, where, send, recv, send_sem, recv_sem).wait_send()

    face_args = (face_send, face_recv, face_s, face_r)
    stress_args = (stress_send, stress_recv, stress_s, stress_r)

    def all_copy(i, peer, send, recv, height, pitch, send_sem, recv_sem):
        return pltpu.make_async_remote_copy(
            src_ref=send.at[pl.ds(pl.multiple_of(peer * pitch, 8), height), :],
            dst_ref=recv.at[pl.ds(pl.multiple_of(me * pitch, 8), height), :],
            send_sem=send_sem.at[i],
            recv_sem=recv_sem.at[i],
            device_id={"yz": peer},
            device_id_type=MESH,
        )

    def all_start(send, recv, height, pitch, send_sem, recv_sem):
        for i, peer, _ in peers:
            all_copy(i, peer, send, recv, height, pitch, send_sem, recv_sem).start()

    def all_wait(send, recv, height, pitch, send_sem, recv_sem):
        for i, _, source in peers:
            pltpu.make_async_remote_copy(
                src_ref=send.at[pl.ds(pl.multiple_of(source * pitch, 8), height), :],
                dst_ref=recv.at[pl.ds(pl.multiple_of(source * pitch, 8), height), :],
                send_sem=send_sem.at[i],
                recv_sem=recv_sem.at[i],
                device_id={"yz": source},
                device_id_type=MESH,
            ).wait_recv()

    def all_sent(send, recv, height, pitch, send_sem, recv_sem):
        for i, peer, _ in peers:
            all_copy(i, peer, send, recv, height, pitch, send_sem, recv_sem).wait_send()

    pay_args = (out_ref, in_ref, SENT * cap, rows, out_s, out_r)
    back_args = (back_send, back_recv, 3 * cap, back_rows, back_s, back_r)

    for load in loads:
        load.wait()

    for c in range(4):
        grid = flow.at[c] if c < 3 else heat
        face_send[0, c] = grid[pl.ds(0, Y), :]
        face_send[1, c] = grid[pl.ds((X - 1) * Y, Y), :]
        face_send[2, c] = grid[pl.ds(0, X, stride=Y), :]
        face_send[3, c] = grid[pl.ds(Y - 1, X, stride=Y), :]

    iota = functools.partial(lax.broadcasted_iota, jnp.int32)
    eye = iota((moving, moving), 0) == iota((moving, moving), 1)
    target_row = target[...]
    target_col = jnp.sum(jnp.where(eye, target_row, 0), axis=1, keepdims=True)
    earlier = (target_col == target_row) & (iota((moving, moving), 0) < iota((moving, moving), 1))
    rank = jnp.sum(jnp.where(earlier, 1, 0), axis=0, keepdims=True)
    slot_row = rank * n + target_row
    slot_hot = onehot(iota((received, moving), 0) == slot_row)
    block_hot = onehot(iota((blocks, moving), 0) == table[...])
    from_block = dot_last(slot_hot.astype(BF16), block_hot.astype(BF16)).astype(BF16)
    to_block = dot_last(block_hot.astype(BF16), slot_hot.astype(BF16))
    moved = jnp.sum(to_block, axis=1, keepdims=True) > 0.5
    to_block = to_block.astype(BF16)
    pencil_out = jnp.sum(slot_hot * entered[...].astype(F32), axis=1, keepdims=True)

    home_t = onehot(iota((pencils, blocks), 0) == home[...])
    home_hot = home_t.T.astype(BF16)
    home_t = home_t.astype(BF16)
    live = onehot(iota((slots, blocks), 0) < tally[...]).T

    where = cells[...]
    u = [lanes(pick(home_hot, flow[c]), where) for c in range(3)]
    temp = lanes(pick(home_hot, heat[...]), where)
    spread = jnp.sqrt((1.0 - DECAY * DECAY) * temp)
    weight = mass[...] * live
    first = [drift(speed[c], u[c], spread, noise[c]) for c in range(3)]
    sent = [pick(from_block, first[c]) for c in range(3)]
    sent.append(pick(from_block, weight))
    sent += [pick(from_block, noise[3 + c]) for c in range(3)]
    sent.append(dot(from_block, where.astype(F32).astype(BF16)))
    sent.append(jnp.broadcast_to(pencil_out, (received, slots)))
    for c in range(SENT):
        for j in range(cap):
            out_ref[pl.ds(c * cap + j, n, stride=rows), :] = sent[c][j * n : (j + 1) * n]

    expected = n - 1 + jnp.where(gx > 0, 1, 0) + jnp.where(gx < n_gx - 1, 1, 0)
    pl.semaphore_wait(barrier, expected)
    all_start(*pay_args)
    faces_start(*face_args)
    own = pl.ds(pl.multiple_of(me * rows, 8), rows)
    in_ref[own, :] = out_ref[own, :]

    second = [drift(first[c], u[c], spread, noise[3 + c]) for c in range(3)]
    for c in range(3):
        second_ref[c] = second[c]
    put_terms(v_ref, blocks, jnp.where(moved, 0.0, weight), second)
    deposit(blocks, math.gcd(blocks, UNROLL), v_ref, cells, pb_ref)
    for k in range(MOMENTS):
        moments[k] = pick(home_t, pb_ref[pl.ds(k, blocks, stride=PITCH), :])

    all_wait(*pay_args)
    got = [
        jnp.concatenate(
            [in_ref[pl.ds(c * cap + j, n, stride=rows), :] for j in range(cap)], axis=0
        )
        for c in range(SENT)
    ]
    where_a = got[7].astype(jnp.int32)
    cells_a[...] = where_a
    pencil_hot = onehot(got[8][:, :pencils].astype(jnp.int32) == iota((received, pencils), 1))
    pencil_t = pencil_hot.T.astype(BF16)
    pencil_hot = pencil_hot.astype(BF16)
    u_a = [lanes(pick(pencil_hot, flow[c]), where_a) for c in range(3)]
    temp_a = lanes(pick(pencil_hot, heat[...]), where_a)
    spread_a = jnp.sqrt((1.0 - DECAY * DECAY) * temp_a)
    second_a = [drift(got[c], u_a[c], spread_a, got[4 + c]) for c in range(3)]
    put_terms(v_ref, received, got[3], second_a)
    deposit(received, math.gcd(received, UNROLL), v_ref, cells_a, pb_ref)
    for k in range(MOMENTS - 1, -1, -1):
        total = moments[k] + pick(pencil_t, pb_ref[pl.ds(k, received, stride=PITCH), :])
        moments[k] = total
        if k >= 4:
            s = k - 4
            stress_send[0, s] = total[:Y]
            stress_send[1, s] = total[pencils - Y :]
            stress_send[2, s] = moments[k, pl.ds(0, X, stride=Y), :]
            stress_send[3, s] = moments[k, pl.ds(Y - 1, X, stride=Y), :]
    faces_start(*stress_args)

    lane = iota((pencils, Z), 1)

    def along_z(x, step):
        if step > 0:
            return jnp.where(lane == Z - 1, 0.0, pltpu.roll(x, Z - 1, 1))
        return jnp.where(lane == 0, 0.0, pltpu.roll(x, 1, 1))

    def fill(slot, value, halo, c):
        wide[slot, 1 : X + 1, 8 : 8 + Y, :] = value.reshape(X, Y, Z)
        wide[slot, 0, 8 : 8 + Y, :] = halo[0, c]
        wide[slot, X + 1, 8 : 8 + Y, :] = halo[1, c]
        for x in range(X):
            wide[slot, x + 1, 7:8, :] = halo[2, c, x : x + 1]
            wide[slot, x + 1, 8 + Y : 9 + Y, :] = halo[3, c, x : x + 1]

    def along_x(slot, step):
        return wide[slot, 1 + step : 1 + step + X, 8 : 8 + Y, :].reshape(pencils, Z)

    def along_y(slot, step):
        return wide[slot, 1 : X + 1, 8 + step : 8 + step + Y, :].reshape(pencils, Z)

    faces_wait(*face_args)
    f = [flow[0], flow[1], flow[2], heat[...]]
    base = []
    for c in range(4):
        fill(c, f[c], face_recv, c)
        smooth = along_x(c, 1) + along_x(c, -1) + along_y(c, 1) + along_y(c, -1)
        smooth = smooth + along_z(f[c], 1) + along_z(f[c], -1) - 6.0 * f[c]
        base.append(f[c] + VISCOSITY * smooth)
    density = moments[0]
    momentum = [moments[1 + c] for c in range(3)]
    for c in range(3):
        base[c] = base[c] + COUPLING * (momentum[c] - density * f[c])
    dots = momentum[0] * f[0] + momentum[1] * f[1] + momentum[2] * f[2]
    squares = f[0] * f[0] + f[1] * f[1] + f[2] * f[2]
    energy = (moments[4] + moments[7] + moments[9] - 2.0 * dots + density * squares) / 3.0
    fields_out[3] = base[3] + COUPLING * (energy - density * f[3])
    stress = [moments[4 + s] for s in range(6)]
    slope_z = [along_z(stress[s], 1) - along_z(stress[s], -1) for s in (2, 4, 5)]

    faces_wait(*stress_args)
    for s in range(6):
        if s < 5:
            fill(4 + s, stress[s], stress_recv, s)
    fresh = []
    for row in range(3):
        sx, sy, _ = PAIR_INDEX[row]
        slope = along_x(4 + sx, 1) - along_x(4 + sx, -1) + slope_z[row]
        slope = slope + along_y(4 + sy, 1) - along_y(4 + sy, -1)
        value = base[row] - (0.5 * STRESS_GAIN) * slope
        fields_out[row] = value
        fresh.append(split3(value))

    def sampled(hot, c):
        return dot(hot, fresh[c][0]) + dot(hot, fresh[c][1]) + dot(hot, fresh[c][2])

    for c in range(3):
        w = lanes(sampled(pencil_hot, c), where_a)
        third = second_a[c] + RELAXATION * (w - second_a[c])
        for j in range(cap):
            back_send[pl.ds(c * cap + j, n, stride=back_rows), :] = third[j * n : (j + 1) * n]
    all_start(*back_args)
    own = pl.ds(pl.multiple_of(me * back_rows, 8), back_rows)
    back_recv[own, :] = back_send[own, :]
    for c in range(3):
        w = lanes(sampled(home_hot, c), where)
        now = second_ref[c]
        second_ref[c] = live * (now + RELAXATION * (w - now))
    all_wait(*back_args)
    for c in range(3):
        returned = jnp.concatenate(
            [back_recv[pl.ds(c * cap + j, n, stride=back_rows), :] for j in range(cap)], axis=0
        )
        speed_out[c] = jnp.where(moved, live * pick(to_block, returned), second_ref[c])

    all_sent(*pay_args)
    faces_sent(*face_args)
    faces_sent(*stress_args)
    all_sent(*back_args)


def put_out(fields, velocity, fields_out, velocity_out, sems):
    copies = (
        pltpu.make_async_copy(fields, fields_out, sems.at[0]),
        pltpu.make_async_copy(velocity, velocity_out, sems.at[1]),
    )
    for copy in copies:
        copy.start()
    for copy in copies:
        copy.wait()


def shards(
    flow_speed_field,
    thermal_field,
    walker_speed_vectors,
    walker_statistical_mass,
    gaussian_samples,
    walker_strip_position,
    group_active_tally,
    group_resident_strip,
    migrating_group_table,
    target_processor_slot,
    entered_strip_slot,
):
    n = lax.axis_size("yz")
    n_gx = lax.axis_size("gx")
    X, Y, Z = thermal_field.shape
    blocks, slots = walker_statistical_mass.shape
    moving = migrating_group_table.shape[0]
    cap = 2 * moving // n
    received = n * cap
    rows = -(-SENT * cap // 8) * 8
    back_rows = -(-3 * cap // 8) * 8
    operands = (
        flow_speed_field.reshape(3, X * Y, Z),
        thermal_field.reshape(X * Y, Z),
        walker_speed_vectors,
        walker_statistical_mass,
        gaussian_samples.reshape(6, blocks, slots),
        walker_strip_position,
        group_active_tally.reshape(1, blocks),
        group_resident_strip.reshape(1, blocks),
        migrating_group_table.reshape(1, moving),
        target_processor_slot.reshape(1, moving),
        entered_strip_slot.reshape(1, moving),
    )
    vmem = pl.BlockSpec(memory_space=pltpu.VMEM)
    fields, velocity = pl.pallas_call(
        functools.partial(kernel, n, n_gx, (X, Y, Z)),
        out_shape=(
            pltpu.VMEM((4, X * Y, Z), F32),
            pltpu.VMEM((3, blocks, slots), F32),
        ),
        in_specs=[pl.BlockSpec(memory_space=pltpu.HBM)] * 11,
        out_specs=(vmem, vmem),
        scratch_shapes=[pltpu.VMEM(x.shape, x.dtype) for x in operands]
        + [pltpu.SemaphoreType.DMA((11,))]
        + [
            pltpu.VMEM((max(blocks, received) * PITCH, slots), F32),
            pltpu.VMEM((max(blocks, received) * PITCH, Z), F32),
            pltpu.VMEM((3, blocks, slots), F32),
            pltpu.VMEM((received, slots), jnp.int32),
            pltpu.VMEM((MOMENTS, X * Y, Z), F32),
            pltpu.VMEM((9, X + 2, 24, Z), F32),
            pltpu.VMEM((4, 4, 8, Z), F32),
            pltpu.VMEM((4, 4, 8, Z), F32),
            pltpu.VMEM((4, 6, 8, Z), F32),
            pltpu.VMEM((4, 6, 8, Z), F32),
            pltpu.VMEM((n * rows, slots), F32),
            pltpu.VMEM((n * rows, slots), F32),
            pltpu.VMEM((n * back_rows, slots), F32),
            pltpu.VMEM((n * back_rows, slots), F32),
            pltpu.SemaphoreType.DMA((n,)),
            pltpu.SemaphoreType.DMA((n,)),
            pltpu.SemaphoreType.DMA((4,)),
            pltpu.SemaphoreType.DMA((4,)),
            pltpu.SemaphoreType.DMA((4,)),
            pltpu.SemaphoreType.DMA((4,)),
            pltpu.SemaphoreType.DMA((n,)),
            pltpu.SemaphoreType.DMA((n,)),
        ],
        compiler_params=pltpu.CompilerParams(
            collective_id=0, has_side_effects=True, vmem_limit_bytes=32 * 1024 * 1024
        ),
    )(*(pltpu.with_memory_space_constraint(x, pltpu.HBM) for x in operands))
    hbm = pl.BlockSpec(memory_space=pltpu.HBM)
    fields, velocity = pl.pallas_call(
        put_out,
        out_shape=(
            jax.ShapeDtypeStruct((4, X * Y, Z), F32),
            jax.ShapeDtypeStruct((3, blocks, slots), F32),
        ),
        in_specs=[vmem, vmem],
        out_specs=(hbm, hbm),
        scratch_shapes=[pltpu.SemaphoreType.DMA((2,))],
        compiler_params=pltpu.CompilerParams(vmem_limit_bytes=32 * 1024 * 1024),
    )(fields, velocity)
    return fields.reshape(4, X, Y, Z), velocity


def solution(mesh):
    return jax.shard_map(
        shards,
        mesh=mesh,
        in_specs=(
            P(None, "gx", "yz", None),
            P("gx", "yz", None),
            P(None, ("gx", "yz"), None),
            P(("gx", "yz"), None),
            P(None, None, ("gx", "yz"), None),
            P(("gx", "yz"), None),
            P(("gx", "yz")),
            P(("gx", "yz")),
            P(("gx", "yz")),
            P(("gx", "yz"), None),
            P(("gx", "yz")),
        ),
        out_specs=(P(None, "gx", "yz", None), P(None, ("gx", "yz"), None)),
        check_vma=False,
    )
```

profile of v0, /device:TPU:0, one launch (start us, length us, event | category | flops | bytes accessed | tf_op | source)
XLA Modules:
  0.0 21.6 jit_solution(9408012251899976251)
XLA Ops:
  0.6 20.2 %shard_map.122 = (f32[4,64,128]{2,1,0:T(8,128)S(1)}, f32[3,128,128]{2,1,0:T(8,128)S(1)}) custom-call(f32[3,64,128]{2,1,0:T(8,128)} %bitcast.10, f32[64,128]{1,0:T(8,128)} %bitcast.11, f32[3,128,128]{2,1,0:T(8,128)} %refs_2_.1, f32[128,128]{1,0:T(8,128)} %refs_3_.1, f32[6,128,128]{2,1,0:T(8,128)} %bitcast.9, s32[128,128]{1,0:T(8,128)} %refs_5_.1, ...), custom_call_target="tpu_custom_call" | custom-call | tf_op jit(solution)/shard_map/pallas_call | solution.py:448
  20.9 0.7 %shard_map.123 = (f32[4,64,128]{2,1,0:T(8,128)}, f32[3,128,128]{2,1,0:T(8,128)}) custom-call(f32[4,64,128]{2,1,0:T(8,128)S(1)} %get-tuple-element.6.fields, f32[3,128,128]{2,1,0:T(8,128)S(1)} %get-tuple-element.7.velocity), custom_call_target="tpu_custom_call" | custom-call | tf_op jit(solution)/shard_map/pallas_call | solution.py:487
where the time goes:
time: 21.7 us; the launch traced here: 21.6 us
  Pallas kernels  20.9 us (96%)
  between operations  0.64 us (3%)
    pallas_call x1, Pallas kernels, shards(): pl.pallas_call(functools.partial(kernel, n, n_gx, (X, Y, Z)), out_shape=(...  20.2 us
    pallas_call x1, Pallas kernels, shards(): pl.pallas_call(put_out, out_shape=(jax.ShapeDtypeStruct((4, X * Y, Z), F3...  0.74 us

commit v1 on v0

--- a/solution.py
+++ b/solution.py
@@ -16,21 +16,20 @@
 PAIRS = ((0, 0), (0, 1), (0, 2), (1, 1), (1, 2), (2, 2))
 PAIR_INDEX = ((0, 1, 2), (1, 3, 4), (2, 4, 5))
 MOMENTS = 10
-PITCH = 16
-SENT = 9
-UNROLL = 32
-LOAD_ORDER = (6, 7, 8, 9, 10, 0, 1, 5, 2, 3, 4)
+PITCH = 24
+SENT = 8
+UNROLL = 16
+LOAD_ORDER = (8, 9, 10, 7, 6, 0, 1, 5, 3, 4, 2)
+X_FACE = tuple(row[0] for row in PAIR_INDEX)
+Y_FACE = tuple(row[1] for row in PAIR_INDEX)
 MESH = pl.DeviceIdType.MESH
 BF16 = jnp.bfloat16
 F32 = jnp.float32
 
 
-def split3(x):
+def split(x):
     high = x.astype(BF16)
-    rest = x - high.astype(F32)
-    mid = rest.astype(BF16)
-    low = (rest - mid.astype(F32)).astype(BF16)
-    return high, mid, low
+    return high, (x - high.astype(F32)).astype(BF16)
 
 
 def dot(a, b):
@@ -41,9 +40,12 @@
     return lax.dot_general(a, b, (((1,), (1,)), ((), ())), preferred_element_type=F32)
 
 
-def pick(onehot, x):
-    high, mid, low = split3(x)
-    return dot(onehot, high) + dot(onehot, mid) + dot(onehot, low)
+def twice(x, axis):
+    return jnp.concatenate([x, x], axis=axis)
+
+
+def pick(onehot_twice, x):
+    return dot(onehot_twice, jnp.concatenate(split(x), axis=0))
 
 
 def lanes(x, index):
@@ -58,32 +60,53 @@
     return u + DECAY * (start - u) + spread * noise
 
 
-def deposit(count, unroll, v_ref, cells_ref, pb_ref):
+def deposit(count, v_ref, cells_ref, pb_ref):
     width = v_ref.shape[1]
     slots = cells_ref.shape[1]
+    half = count // 2
+    unroll = math.gcd(half, UNROLL)
     where = lax.broadcasted_iota(jnp.int32, (width, slots), 0)
+    none = jnp.zeros((8, slots), F32)
+    mine = lax.broadcasted_iota(jnp.int32, (8, slots), 0) < MOMENTS - 8
 
     def some(step, carry):
         for t in range(unroll):
             n = step * unroll + t
-            row = pl.ds(pl.multiple_of(n * PITCH, PITCH), PITCH)
-            lhs = jnp.concatenate(split3(v_ref[row, :]), axis=0)
-            hot = onehot(cells_ref[pl.ds(n, 1), :] == where).astype(BF16)
+            start = pl.multiple_of(n * 2 * PITCH, 2 * PITCH)
+            rows = [v_ref[pl.ds(start + 8 * part, 8), :] for part in range(6)]
+            left = [rows[0], jnp.where(mine, rows[1], 0.0), none, rows[3], jnp.where(mine, rows[4], 0.0), none]
+            right = [none, jnp.where(mine, 0.0, rows[1]), rows[2], none, jnp.where(mine, 0.0, rows[4]), rows[5]]
+            lhs = jnp.concatenate(
+                [jnp.concatenate(side, axis=0).astype(BF16) for side in (left, right)], axis=1
+            )
+            hot = jnp.concatenate(
+                [onehot(cells_ref[pl.ds(n + block, 1), :] == where).astype(BF16) for block in (0, half)], axis=1
+            )
             out = dot_last(lhs, hot)
-            pb_ref[row, :] = out[:PITCH] + out[PITCH : 2 * PITCH] + out[2 * PITCH :]
+            pb_ref[pl.ds(pl.multiple_of(n * PITCH, 8), PITCH), :] = out[:PITCH] + out[PITCH:]
         return carry
 
-    lax.fori_loop(0, count // unroll, some, 0)
+    lax.fori_loop(0, half // unroll, some, 0)
 
 
 def put_terms(v_ref, count, weight, second):
-    terms = (
-        [weight]
-        + [weight * second[row] for row in range(3)]
-        + [weight * second[one] * second[two] for one, two in PAIRS]
+    half = count // 2
+    weighted = [weight * second[row] for row in range(3)]
+    terms = [weight] + weighted + [weighted[one] * second[two] for one, two in PAIRS]
+    for k, term in enumerate(terms):
+        high = term.astype(BF16).astype(F32)
+        for part, value in enumerate((high, term - high)):
+            for block in range(2):
+                v_ref[pl.ds(part * PITCH + block * MOMENTS + k, half, stride=2 * PITCH), :] = value[
+                    block * half : (block + 1) * half
+                ]
+
+
+def deposited(pb_ref, count, k):
+    half = count // 2
+    return jnp.concatenate(
+        [pb_ref[pl.ds(block * MOMENTS + k, half, stride=PITCH), :] for block in range(2)], axis=0
     )
-    for k, term in enumerate(terms):
-        v_ref[pl.ds(k, count, stride=PITCH), :] = term
 
 
 def kernel(
@@ -225,12 +248,43 @@
         for i, peer, _ in peers:
             all_copy(i, peer, send, recv, height, pitch, send_sem, recv_sem).wait_send()
 
-    pay_args = (out_ref, in_ref, SENT * cap, rows, out_s, out_r)
+    pay_args = (out_ref, in_ref, SENT * cap + 1, rows, out_s, out_r)
     back_args = (back_send, back_recv, 3 * cap, back_rows, back_s, back_r)
 
-    for load in loads:
-        load.wait()
-
+    def landed(*which):
+        for i in which:
+            loads[i].wait()
+
+    landed(8, 9, 10, 7, 6)
+    iota = functools.partial(lax.broadcasted_iota, jnp.int32)
+
+    def folded(shape, axis, period):
+        place = iota(shape, axis)
+        return jnp.where(place < period, place, place - period)
+
+    eye = iota((moving, moving), 0) == iota((moving, moving), 1)
+    target_row = target[...]
+    target_col = jnp.sum(jnp.where(eye, target_row, 0), axis=1, keepdims=True)
+    earlier = (target_col == target_row) & (iota((moving, moving), 0) < iota((moving, moving), 1))
+    rank = jnp.sum(jnp.where(earlier, 1, 0), axis=0, keepdims=True)
+    slot_row = rank * n + target_row
+    slot_hot = onehot(folded((2 * received, moving), 0, received) == slot_row)
+    block_hot = onehot(iota((blocks, moving), 0) == table[...]).astype(BF16)
+    from_block = dot_last(slot_hot[:received].astype(BF16), block_hot).astype(BF16)
+    from_twice = twice(from_block, 1)
+    to_block = dot_last(block_hot, slot_hot.astype(BF16))
+    moved = jnp.sum(to_block, axis=1, keepdims=True) > 0.5
+    to_block = to_block.astype(BF16)
+    pencil_out = jnp.sum(slot_hot[:received] * entered[...].astype(F32), axis=1, keepdims=True)
+
+    home_t = onehot(folded((2 * pencils, blocks), 0, pencils) == home[...])
+    home_hot = home_t.T.astype(BF16)
+    home_t = twice(home_t[:pencils].astype(BF16), 1)
+    live = onehot(iota((slots, blocks), 0) < tally[...]).T
+
+    landed(0, 1)
+    u = [pick(home_hot, flow[c]) for c in range(3)]
+    temp = pick(home_hot, heat[...])
     for c in range(4):
         grid = flow.at[c] if c < 3 else heat
         face_send[0, c] = grid[pl.ds(0, Y), :]
@@ -238,40 +292,32 @@
         face_send[2, c] = grid[pl.ds(0, X, stride=Y), :]
         face_send[3, c] = grid[pl.ds(Y - 1, X, stride=Y), :]
 
-    iota = functools.partial(lax.broadcasted_iota, jnp.int32)
-    eye = iota((moving, moving), 0) == iota((moving, moving), 1)
-    target_row = target[...]
-    target_col = jnp.sum(jnp.where(eye, target_row, 0), axis=1, keepdims=True)
-    earlier = (target_col == target_row) & (iota((moving, moving), 0) < iota((moving, moving), 1))
-    rank = jnp.sum(jnp.where(earlier, 1, 0), axis=0, keepdims=True)
-    slot_row = rank * n + target_row
-    slot_hot = onehot(iota((received, moving), 0) == slot_row)
-    block_hot = onehot(iota((blocks, moving), 0) == table[...])
-    from_block = dot_last(slot_hot.astype(BF16), block_hot.astype(BF16)).astype(BF16)
-    to_block = dot_last(block_hot.astype(BF16), slot_hot.astype(BF16))
-    moved = jnp.sum(to_block, axis=1, keepdims=True) > 0.5
-    to_block = to_block.astype(BF16)
-    pencil_out = jnp.sum(slot_hot * entered[...].astype(F32), axis=1, keepdims=True)
-
-    home_t = onehot(iota((pencils, blocks), 0) == home[...])
-    home_hot = home_t.T.astype(BF16)
-    home_t = home_t.astype(BF16)
-    live = onehot(iota((slots, blocks), 0) < tally[...]).T
-
+    landed(5, 3)
     where = cells[...]
-    u = [lanes(pick(home_hot, flow[c]), where) for c in range(3)]
-    temp = lanes(pick(home_hot, heat[...]), where)
-    spread = jnp.sqrt((1.0 - DECAY * DECAY) * temp)
+    u = [lanes(u[c], where) for c in range(3)]
+    spread = jnp.sqrt((1.0 - DECAY * DECAY) * lanes(temp, where))
     weight = mass[...] * live
+
+    def send_row(c, value):
+        for j in range(cap):
+            out_ref[pl.ds(c * cap + j, n, stride=rows), :] = value[j * n : (j + 1) * n]
+
+    send_row(6, pick(from_twice, weight))
+    send_row(7, dot(from_block, where.astype(F32).astype(BF16)))
+    group = lax.div(iota((n, slots), 1), slots // cap)
+    pencil_row = jnp.broadcast_to(pencil_out[:n], (n, slots))
+    for j in range(1, cap):
+        pencil_row = jnp.where(group == j, pencil_out[j * n : (j + 1) * n], pencil_row)
+    out_ref[pl.ds(SENT * cap, n, stride=rows), :] = pencil_row
+
+    landed(4)
+    for c in range(3):
+        send_row(3 + c, pick(from_twice, noise[3 + c]))
+
+    landed(2)
     first = [drift(speed[c], u[c], spread, noise[c]) for c in range(3)]
-    sent = [pick(from_block, first[c]) for c in range(3)]
-    sent.append(pick(from_block, weight))
-    sent += [pick(from_block, noise[3 + c]) for c in range(3)]
-    sent.append(dot(from_block, where.astype(F32).astype(BF16)))
-    sent.append(jnp.broadcast_to(pencil_out, (received, slots)))
-    for c in range(SENT):
-        for j in range(cap):
-            out_ref[pl.ds(c * cap + j, n, stride=rows), :] = sent[c][j * n : (j + 1) * n]
+    for c in range(3):
+        send_row(c, pick(from_twice, first[c]))
 
     expected = n - 1 + jnp.where(gx > 0, 1, 0) + jnp.where(gx < n_gx - 1, 1, 0)
     pl.semaphore_wait(barrier, expected)
@@ -284,9 +330,9 @@
     for c in range(3):
         second_ref[c] = second[c]
     put_terms(v_ref, blocks, jnp.where(moved, 0.0, weight), second)
-    deposit(blocks, math.gcd(blocks, UNROLL), v_ref, cells, pb_ref)
+    deposit(blocks, v_ref, cells, pb_ref)
     for k in range(MOMENTS):
-        moments[k] = pick(home_t, pb_ref[pl.ds(k, blocks, stride=PITCH), :])
+        moments[k] = pick(home_t, deposited(pb_ref, blocks, k))
 
     all_wait(*pay_args)
     got = [
@@ -297,25 +343,35 @@
     ]
     where_a = got[7].astype(jnp.int32)
     cells_a[...] = where_a
-    pencil_hot = onehot(got[8][:, :pencils].astype(jnp.int32) == iota((received, pencils), 1))
-    pencil_t = pencil_hot.T.astype(BF16)
+    pencil_row = in_ref[pl.ds(SENT * cap, n, stride=rows), :]
+    pencil_in = jnp.concatenate(
+        [lanes(pencil_row, jnp.full((n, slots), j * (slots // cap), jnp.int32)) for j in range(cap)], axis=0
+    ).astype(jnp.int32)
+    pencil_hot = onehot(pencil_in[:, : 2 * pencils] == folded((received, 2 * pencils), 1, pencils))
+    pencil_t = twice(pencil_hot[:, :pencils], 0).T.astype(BF16)
     pencil_hot = pencil_hot.astype(BF16)
     u_a = [lanes(pick(pencil_hot, flow[c]), where_a) for c in range(3)]
     temp_a = lanes(pick(pencil_hot, heat[...]), where_a)
     spread_a = jnp.sqrt((1.0 - DECAY * DECAY) * temp_a)
-    second_a = [drift(got[c], u_a[c], spread_a, got[4 + c]) for c in range(3)]
-    put_terms(v_ref, received, got[3], second_a)
-    deposit(received, math.gcd(received, UNROLL), v_ref, cells_a, pb_ref)
-    for k in range(MOMENTS - 1, -1, -1):
-        total = moments[k] + pick(pencil_t, pb_ref[pl.ds(k, received, stride=PITCH), :])
-        moments[k] = total
-        if k >= 4:
-            s = k - 4
-            stress_send[0, s] = total[:Y]
-            stress_send[1, s] = total[pencils - Y :]
-            stress_send[2, s] = moments[k, pl.ds(0, X, stride=Y), :]
-            stress_send[3, s] = moments[k, pl.ds(Y - 1, X, stride=Y), :]
+    second_a = [drift(got[c], u_a[c], spread_a, got[3 + c]) for c in range(3)]
+    put_terms(v_ref, received, got[6], second_a)
+    deposit(received, v_ref, cells_a, pb_ref)
+
+    def total(k):
+        moments[k] = moments[k] + pick(pencil_t, deposited(pb_ref, received, k))
+
+    for k in range(4, MOMENTS):
+        total(k)
+    for row in range(3):
+        k = 4 + X_FACE[row]
+        stress_send[0, row] = moments[k, pl.ds(0, Y), :]
+        stress_send[1, row] = moments[k, pl.ds(pencils - Y, Y), :]
+        k = 4 + Y_FACE[row]
+        stress_send[2, row] = moments[k, pl.ds(0, X, stride=Y), :]
+        stress_send[3, row] = moments[k, pl.ds(Y - 1, X, stride=Y), :]
     faces_start(*stress_args)
+    for k in range(4):
+        total(k)
 
     lane = iota((pencils, Z), 1)
 
@@ -324,10 +380,14 @@
             return jnp.where(lane == Z - 1, 0.0, pltpu.roll(x, Z - 1, 1))
         return jnp.where(lane == 0, 0.0, pltpu.roll(x, 1, 1))
 
-    def fill(slot, value, halo, c):
+    def fill(slot, value):
         wide[slot, 1 : X + 1, 8 : 8 + Y, :] = value.reshape(X, Y, Z)
+
+    def edge_x(slot, halo, c):
         wide[slot, 0, 8 : 8 + Y, :] = halo[0, c]
         wide[slot, X + 1, 8 : 8 + Y, :] = halo[1, c]
+
+    def edge_y(slot, halo, c):
         for x in range(X):
             wide[slot, x + 1, 7:8, :] = halo[2, c, x : x + 1]
             wide[slot, x + 1, 8 + Y : 9 + Y, :] = halo[3, c, x : x + 1]
@@ -342,7 +402,9 @@
     f = [flow[0], flow[1], flow[2], heat[...]]
     base = []
     for c in range(4):
-        fill(c, f[c], face_recv, c)
+        fill(c, f[c])
+        edge_x(c, face_recv, c)
+        edge_y(c, face_recv, c)
         smooth = along_x(c, 1) + along_x(c, -1) + along_y(c, 1) + along_y(c, -1)
         smooth = smooth + along_z(f[c], 1) + along_z(f[c], -1) - 6.0 * f[c]
         base.append(f[c] + VISCOSITY * smooth)
@@ -355,26 +417,26 @@
     energy = (moments[4] + moments[7] + moments[9] - 2.0 * dots + density * squares) / 3.0
     fields_out[3] = base[3] + COUPLING * (energy - density * f[3])
     stress = [moments[4 + s] for s in range(6)]
-    slope_z = [along_z(stress[s], 1) - along_z(stress[s], -1) for s in (2, 4, 5)]
+    for s in range(5):
+        fill(4 + s, stress[s])
+    for row in range(3):
+        sz = stress[PAIR_INDEX[row][2]]
+        base[row] = base[row] - (0.5 * STRESS_GAIN) * (along_z(sz, 1) - along_z(sz, -1))
 
     faces_wait(*stress_args)
-    for s in range(6):
-        if s < 5:
-            fill(4 + s, stress[s], stress_recv, s)
+    for row in range(3):
+        edge_x(4 + X_FACE[row], stress_recv, row)
+        edge_y(4 + Y_FACE[row], stress_recv, row)
     fresh = []
     for row in range(3):
-        sx, sy, _ = PAIR_INDEX[row]
-        slope = along_x(4 + sx, 1) - along_x(4 + sx, -1) + slope_z[row]
-        slope = slope + along_y(4 + sy, 1) - along_y(4 + sy, -1)
+        sx, sy = 4 + X_FACE[row], 4 + Y_FACE[row]
+        slope = along_x(sx, 1) - along_x(sx, -1) + along_y(sy, 1) - along_y(sy, -1)
         value = base[row] - (0.5 * STRESS_GAIN) * slope
         fields_out[row] = value
-        fresh.append(split3(value))
-
-    def sampled(hot, c):
-        return dot(hot, fresh[c][0]) + dot(hot, fresh[c][1]) + dot(hot, fresh[c][2])
-
-    for c in range(3):
-        w = lanes(sampled(pencil_hot, c), where_a)
+        fresh.append(jnp.concatenate(split(value), axis=0))
+
+    for c in range(3):
+        w = lanes(dot(pencil_hot, fresh[c]), where_a)
         third = second_a[c] + RELAXATION * (w - second_a[c])
         for j in range(cap):
             back_send[pl.ds(c * cap + j, n, stride=back_rows), :] = third[j * n : (j + 1) * n]
@@ -382,7 +444,7 @@
     own = pl.ds(pl.multiple_of(me * back_rows, 8), back_rows)
     back_recv[own, :] = back_send[own, :]
     for c in range(3):
-        w = lanes(sampled(home_hot, c), where)
+        w = lanes(dot(home_hot, fresh[c]), where)
         now = second_ref[c]
         second_ref[c] = live * (now + RELAXATION * (w - now))
     all_wait(*back_args)
@@ -429,7 +491,7 @@
     moving = migrating_group_table.shape[0]
     cap = 2 * moving // n
     received = n * cap
-    rows = -(-SENT * cap // 8) * 8
+    rows = -(-(SENT * cap + 1) // 8) * 8
     back_rows = -(-3 * cap // 8) * 8
     operands = (
         flow_speed_field.reshape(3, X * Y, Z),
@@ -457,15 +519,15 @@
         + [pltpu.SemaphoreType.DMA((11,))]
         + [
             pltpu.VMEM((max(blocks, received) * PITCH, slots), F32),
-            pltpu.VMEM((max(blocks, received) * PITCH, Z), F32),
+            pltpu.VMEM((max(blocks, received) // 2 * PITCH, Z), F32),
             pltpu.VMEM((3, blocks, slots), F32),
             pltpu.VMEM((received, slots), jnp.int32),
             pltpu.VMEM((MOMENTS, X * Y, Z), F32),
             pltpu.VMEM((9, X + 2, 24, Z), F32),
             pltpu.VMEM((4, 4, 8, Z), F32),
             pltpu.VMEM((4, 4, 8, Z), F32),
-            pltpu.VMEM((4, 6, 8, Z), F32),
-            pltpu.VMEM((4, 6, 8, Z), F32),
+            pltpu.VMEM((4, 3, 8, Z), F32),
+            pltpu.VMEM((4, 3, 8, Z), F32),
             pltpu.VMEM((n * rows, slots), F32),
             pltpu.VMEM((n * rows, slots), F32),
             pltpu.VMEM((n * back_rows, slots), F32),

time: 21.7 us -> 21.1 us (0.972)
  Pallas kernels: 20.9 us -> 20.3 us
    pallas_call x1, Pallas kernels: 20.2 us -> 19.6 us  [shards(): pl.pallas_call(functools.partial(kernel, n, n_gx, (X, Y, Z)), out_shape=(...]
where the time goes in v1:
time: 21.1 us; the launch traced here: 21 us
  Pallas kernels  20.3 us (96%)
  between operations  0.64 us (3%)
    pallas_call x1, Pallas kernels, shards(): pl.pallas_call(functools.partial(kernel, n, n_gx, (X, Y, Z)), out_shape=(...  19.6 us
    pallas_call x1, Pallas kernels, shards(): pl.pallas_call(put_out, out_shape=(jax.ShapeDtypeStruct((4, X * Y, Z), F3...  0.74 us

profile of v1, /device:TPU:0, one launch (start us, length us, event | category | flops | bytes accessed | tf_op | source)
XLA Modules:
  0.0 21.0 jit_solution(15308546004164475706)
XLA Ops:
  0.6 19.6 %shard_map.122 = (f32[4,64,128]{2,1,0:T(8,128)S(1)}, f32[3,128,128]{2,1,0:T(8,128)S(1)}) custom-call(f32[3,64,128]{2,1,0:T(8,128)} %bitcast.10, f32[64,128]{1,0:T(8,128)} %bitcast.11, f32[3,128,128]{2,1,0:T(8,128)} %refs_2_.1, f32[128,128]{1,0:T(8,128)} %refs_3_.1, f32[6,128,128]{2,1,0:T(8,128)} %bitcast.9, s32[128,128]{1,0:T(8,128)} %refs_5_.1, ...), custom_call_target="tpu_custom_call" | custom-call | tf_op jit(solution)/shard_map/pallas_call | solution.py:510
  20.2 0.7 %shard_map.123 = (f32[4,64,128]{2,1,0:T(8,128)}, f32[3,128,128]{2,1,0:T(8,128)}) custom-call(f32[4,64,128]{2,1,0:T(8,128)S(1)} %get-tuple-element.6.fields, f32[3,128,128]{2,1,0:T(8,128)S(1)} %get-tuple-element.7.velocity), custom_call_target="tpu_custom_call" | custom-call | tf_op jit(solution)/shard_map/pallas_call | solution.py:549

commit v2 on v1

--- a/solution.py
+++ b/solution.py
@@ -56,11 +56,20 @@
     return jnp.where(condition, 1.0, 0.0)
 
 
+def partner(me, i, n):
+    peer, bit = 0, 1
+    while bit < n:
+        own = lax.rem(lax.div(me, bit), 2)
+        peer = peer + bit * (1 - own if i & bit else own)
+        bit *= 2
+    return peer
+
+
 def drift(start, u, spread, noise):
     return u + DECAY * (start - u) + spread * noise
 
 
-def deposit(count, v_ref, cells_ref, pb_ref):
+def deposit(count, v_ref, cells_ref, pb_ref, first=0, last=None):
     width = v_ref.shape[1]
     slots = cells_ref.shape[1]
     half = count // 2
@@ -86,7 +95,7 @@
             pb_ref[pl.ds(pl.multiple_of(n * PITCH, 8), PITCH), :] = out[:PITCH] + out[PITCH:]
         return carry
 
-    lax.fori_loop(0, half // unroll, some, 0)
+    lax.fori_loop(first, half // unroll if last is None else last, some, 0)
 
 
 def put_terms(v_ref, count, weight, second):
@@ -155,13 +164,16 @@
     back_rows = back_send.shape[0] // n
     gx = lax.axis_index("gx")
     me = lax.axis_index("yz")
-    order = sorted(range(1, n), key=lambda i: abs(2 * i - n))
-    peers = [(i, lax.rem(me + i, n), lax.rem(me + n - i, n)) for i in order]
-    for i in LOAD_ORDER:
-        loads[i].start()
-
+    far = [partner(me, i, n) for i in range(n - 1, n // 2 - 1, -1)]
+    near = [partner(me, i, n) for i in range(n // 2 - 1, 0, -1)]
+    odd = lax.rem(gx, 2)
+    turns = [j + odd * (n - 2 - 2 * j) for j in range(n - 1)]
+    others = [j + lax.div(j + n - me, n) for j in turns]
+    group = received // 2
+    base_a = n // 2 * jnp.minimum(lax.div(me, n // 4), 1)
+    base_b = n // 2 - base_a
     barrier = pltpu.get_barrier_semaphore()
-    for _, peer, _ in peers:
+    for peer in far + near:
         pl.semaphore_signal(barrier, inc=1, device_id={"yz": peer}, device_id_type=MESH)
 
     @pl.when(gx > 0)
@@ -171,6 +183,9 @@
     @pl.when(gx < n_gx - 1)
     def _():
         pl.semaphore_signal(barrier, inc=1, device_id={"gx": gx + 1}, device_id_type=MESH)
+
+    for i in LOAD_ORDER:
+        loads[i].start()
 
     sides = (
         (0, 1, gx > 0, gx == 0, {"gx": gx - 1}),
@@ -219,34 +234,33 @@
     face_args = (face_send, face_recv, face_s, face_r)
     stress_args = (stress_send, stress_recv, stress_s, stress_r)
 
-    def all_copy(i, peer, send, recv, height, pitch, send_sem, recv_sem):
+    def all_copy(peer, source, send, recv, height, pitch, send_sem, recv_sem):
         return pltpu.make_async_remote_copy(
             src_ref=send.at[pl.ds(pl.multiple_of(peer * pitch, 8), height), :],
-            dst_ref=recv.at[pl.ds(pl.multiple_of(me * pitch, 8), height), :],
-            send_sem=send_sem.at[i],
-            recv_sem=recv_sem.at[i],
+            dst_ref=recv.at[pl.ds(pl.multiple_of(source * pitch, 8), height), :],
+            send_sem=send_sem.at[peer],
+            recv_sem=recv_sem.at[source],
             device_id={"yz": peer},
             device_id_type=MESH,
         )
 
-    def all_start(send, recv, height, pitch, send_sem, recv_sem):
-        for i, peer, _ in peers:
-            all_copy(i, peer, send, recv, height, pitch, send_sem, recv_sem).start()
-
-    def all_wait(send, recv, height, pitch, send_sem, recv_sem):
-        for i, _, source in peers:
-            pltpu.make_async_remote_copy(
-                src_ref=send.at[pl.ds(pl.multiple_of(source * pitch, 8), height), :],
-                dst_ref=recv.at[pl.ds(pl.multiple_of(source * pitch, 8), height), :],
-                send_sem=send_sem.at[i],
-                recv_sem=recv_sem.at[i],
-                device_id={"yz": source},
-                device_id_type=MESH,
-            ).wait_recv()
-
-    def all_sent(send, recv, height, pitch, send_sem, recv_sem):
-        for i, peer, _ in peers:
-            all_copy(i, peer, send, recv, height, pitch, send_sem, recv_sem).wait_send()
+    def all_start(peers, *args):
+        for peer in peers:
+            all_copy(peer, me, *args).start()
+
+    def all_wait(peers, *args):
+        for peer in peers:
+            all_copy(peer, peer, *args).wait_recv()
+
+    def half_wait(base, *args):
+        for j in range(n // 2):
+            @pl.when(base + j != me)
+            def _(j=j):
+                all_copy(base + j, base + j, *args).wait_recv()
+
+    def all_sent(peers, *args):
+        for peer in peers:
+            all_copy(peer, me, *args).wait_send()
 
     pay_args = (out_ref, in_ref, SENT * cap + 1, rows, out_s, out_r)
     back_args = (back_send, back_recv, 3 * cap, back_rows, back_s, back_r)
@@ -304,10 +318,10 @@
 
     send_row(6, pick(from_twice, weight))
     send_row(7, dot(from_block, where.astype(F32).astype(BF16)))
-    group = lax.div(iota((n, slots), 1), slots // cap)
+    place = lax.div(iota((n, slots), 1), slots // cap)
     pencil_row = jnp.broadcast_to(pencil_out[:n], (n, slots))
     for j in range(1, cap):
-        pencil_row = jnp.where(group == j, pencil_out[j * n : (j + 1) * n], pencil_row)
+        pencil_row = jnp.where(place == j, pencil_out[j * n : (j + 1) * n], pencil_row)
     out_ref[pl.ds(SENT * cap, n, stride=rows), :] = pencil_row
 
     landed(4)
@@ -321,7 +335,12 @@
 
     expected = n - 1 + jnp.where(gx > 0, 1, 0) + jnp.where(gx < n_gx - 1, 1, 0)
     pl.semaphore_wait(barrier, expected)
-    all_start(*pay_args)
+    late = lax.rem(gx, 2) == 1
+
+    @pl.when(jnp.logical_not(late))
+    def _():
+        all_start(far + near, *pay_args)
+
     faces_start(*face_args)
     own = pl.ds(pl.multiple_of(me * rows, 8), rows)
     in_ref[own, :] = out_ref[own, :]
@@ -330,38 +349,48 @@
     for c in range(3):
         second_ref[c] = second[c]
     put_terms(v_ref, blocks, jnp.where(moved, 0.0, weight), second)
-    deposit(blocks, v_ref, cells, pb_ref)
+    deposit(blocks, v_ref, cells, pb_ref, 0, 3)
+
+    @pl.when(late)
+    def _():
+        all_start(far + near, *pay_args)
+
+    deposit(blocks, v_ref, cells, pb_ref, 3)
     for k in range(MOMENTS):
         moments[k] = pick(home_t, deposited(pb_ref, blocks, k))
 
-    all_wait(*pay_args)
-    got = [
-        jnp.concatenate(
-            [in_ref[pl.ds(c * cap + j, n, stride=rows), :] for j in range(cap)], axis=0
-        )
-        for c in range(SENT)
-    ]
-    where_a = got[7].astype(jnp.int32)
-    cells_a[...] = where_a
-    pencil_row = in_ref[pl.ds(SENT * cap, n, stride=rows), :]
-    pencil_in = jnp.concatenate(
-        [lanes(pencil_row, jnp.full((n, slots), j * (slots // cap), jnp.int32)) for j in range(cap)], axis=0
-    ).astype(jnp.int32)
-    pencil_hot = onehot(pencil_in[:, : 2 * pencils] == folded((received, 2 * pencils), 1, pencils))
-    pencil_t = twice(pencil_hot[:, :pencils], 0).T.astype(BF16)
-    pencil_hot = pencil_hot.astype(BF16)
-    u_a = [lanes(pick(pencil_hot, flow[c]), where_a) for c in range(3)]
-    temp_a = lanes(pick(pencil_hot, heat[...]), where_a)
-    spread_a = jnp.sqrt((1.0 - DECAY * DECAY) * temp_a)
-    second_a = [drift(got[c], u_a[c], spread_a, got[3 + c]) for c in range(3)]
-    put_terms(v_ref, received, got[6], second_a)
-    deposit(received, v_ref, cells_a, pb_ref)
-
-    def total(k):
-        moments[k] = moments[k] + pick(pencil_t, deposited(pb_ref, received, k))
-
+    def migrants(side, base):
+        def taken(row):
+            return in_ref[pl.ds(base * rows + row, n // 2, stride=rows), :]
+
+        got = [jnp.concatenate([taken(c * cap + j) for j in range(cap)], axis=0) for c in range(SENT)]
+        where = got[7].astype(jnp.int32)
+        cells_a[side] = where
+        pencil_row = taken(SENT * cap)
+        pencil = jnp.concatenate(
+            [lanes(pencil_row, jnp.full((n // 2, slots), j * (slots // cap), jnp.int32)) for j in range(cap)], axis=0
+        ).astype(jnp.int32)
+        hot = onehot(pencil[:, : 2 * pencils] == folded((group, 2 * pencils), 1, pencils))
+        hot_t = twice(hot[:, :pencils], 0).T.astype(BF16)
+        hot = hot.astype(BF16)
+        u = [lanes(pick(hot, flow[c]), where) for c in range(3)]
+        spread = jnp.sqrt((1.0 - DECAY * DECAY) * lanes(pick(hot, heat[...]), where))
+        second = [drift(got[c], u[c], spread, got[3 + c]) for c in range(3)]
+        put_terms(v_ref, group, got[6], second)
+        deposit(group, v_ref, cells_a.at[side], pb_ref)
+        return where, hot, hot_t, second
+
+    def total(hot_t, k):
+        moments[k] = moments[k] + pick(hot_t, deposited(pb_ref, group, k))
+
+    half_wait(base_a, *pay_args)
+    where_n, hot_n, hot_t, second_n = migrants(0, base_a)
+    for k in range(MOMENTS):
+        total(hot_t, k)
+    half_wait(base_b, *pay_args)
+    where_f, hot_f, hot_t, second_f = migrants(1, base_b)
     for k in range(4, MOMENTS):
-        total(k)
+        total(hot_t, k)
     for row in range(3):
         k = 4 + X_FACE[row]
         stress_send[0, row] = moments[k, pl.ds(0, Y), :]
@@ -371,7 +400,7 @@
         stress_send[3, row] = moments[k, pl.ds(Y - 1, X, stride=Y), :]
     faces_start(*stress_args)
     for k in range(4):
-        total(k)
+        total(hot_t, k)
 
     lane = iota((pencils, Z), 1)
 
@@ -435,29 +464,35 @@
         fields_out[row] = value
         fresh.append(jnp.concatenate(split(value), axis=0))
 
-    for c in range(3):
-        w = lanes(dot(pencil_hot, fresh[c]), where_a)
-        third = second_a[c] + RELAXATION * (w - second_a[c])
-        for j in range(cap):
-            back_send[pl.ds(c * cap + j, n, stride=back_rows), :] = third[j * n : (j + 1) * n]
-    all_start(*back_args)
+    for base, where_a, hot, second_a in (
+        (base_a, where_n, hot_n, second_n),
+        (base_b, where_f, hot_f, second_f),
+    ):
+        for c in range(3):
+            w = lanes(dot(hot, fresh[c]), where_a)
+            third = second_a[c] + RELAXATION * (w - second_a[c])
+            for j in range(cap):
+                back_send[pl.ds(base * back_rows + c * cap + j, n // 2, stride=back_rows), :] = third[
+                    j * (n // 2) : (j + 1) * (n // 2)
+                ]
+    all_start(others, *back_args)
     own = pl.ds(pl.multiple_of(me * back_rows, 8), back_rows)
     back_recv[own, :] = back_send[own, :]
     for c in range(3):
         w = lanes(dot(home_hot, fresh[c]), where)
         now = second_ref[c]
         second_ref[c] = live * (now + RELAXATION * (w - now))
-    all_wait(*back_args)
+    all_wait(others, *back_args)
     for c in range(3):
         returned = jnp.concatenate(
             [back_recv[pl.ds(c * cap + j, n, stride=back_rows), :] for j in range(cap)], axis=0
         )
         speed_out[c] = jnp.where(moved, live * pick(to_block, returned), second_ref[c])
 
-    all_sent(*pay_args)
+    all_sent(far + near, *pay_args)
     faces_sent(*face_args)
     faces_sent(*stress_args)
-    all_sent(*back_args)
+    all_sent(others, *back_args)
 
 
 def put_out(fields, velocity, fields_out, velocity_out, sems):
@@ -521,7 +556,7 @@
             pltpu.VMEM((max(blocks, received) * PITCH, slots), F32),
             pltpu.VMEM((max(blocks, received) // 2 * PITCH, Z), F32),
             pltpu.VMEM((3, blocks, slots), F32),
-            pltpu.VMEM((received, slots), jnp.int32),
+            pltpu.VMEM((2, received // 2, slots), jnp.int32),
             pltpu.VMEM((MOMENTS, X * Y, Z), F32),
             pltpu.VMEM((9, X + 2, 24, Z), F32),
             pltpu.VMEM((4, 4, 8, Z), F32),

time: 21.1 us -> 20.2 us (0.957)
  Pallas kernels: 20.3 us -> 19.4 us
    pallas_call x1, Pallas kernels: 19.6 us -> 18.7 us  [shards(): pl.pallas_call(functools.partial(kernel, n, n_gx, (X, Y, Z)), out_shape=(...]
where the time goes in v2:
time: 20.2 us; the launch traced here: 20.1 us
  Pallas kernels  19.4 us (96%)
  between operations  0.64 us (3%)
    pallas_call x1, Pallas kernels, shards(): pl.pallas_call(functools.partial(kernel, n, n_gx, (X, Y, Z)), out_shape=(...  18.7 us
    pallas_call x1, Pallas kernels, shards(): pl.pallas_call(put_out, out_shape=(jax.ShapeDtypeStruct((4, X * Y, Z), F3...  0.74 us

profile of v2, /device:TPU:0, one launch (start us, length us, event | category | flops | bytes accessed | tf_op | source)
XLA Modules:
  0.0 20.1 jit_solution(11026867181073144175)
XLA Ops:
  0.6 18.7 %shard_map.122 = (f32[4,64,128]{2,1,0:T(8,128)S(1)}, f32[3,128,128]{2,1,0:T(8,128)S(1)}) custom-call(f32[3,64,128]{2,1,0:T(8,128)} %bitcast.10, f32[64,128]{1,0:T(8,128)} %bitcast.11, f32[3,128,128]{2,1,0:T(8,128)} %refs_2_.1, f32[128,128]{1,0:T(8,128)} %refs_3_.1, f32[6,128,128]{2,1,0:T(8,128)} %bitcast.9, s32[128,128]{1,0:T(8,128)} %refs_5_.1, ...), custom_call_target="tpu_custom_call" | custom-call | tf_op jit(solution)/shard_map/pallas_call | solution.py:545
  19.3 0.7 %shard_map.123 = (f32[4,64,128]{2,1,0:T(8,128)}, f32[3,128,128]{2,1,0:T(8,128)}) custom-call(f32[4,64,128]{2,1,0:T(8,128)S(1)} %get-tuple-element.6.fields, f32[3,128,128]{2,1,0:T(8,128)S(1)} %get-tuple-element.7.velocity), custom_call_target="tpu_custom_call" | custom-call | tf_op jit(solution)/shard_map/pallas_call | solution.py:584

commit v3 on v2

--- a/solution.py
+++ b/solution.py
@@ -19,7 +19,7 @@
 PITCH = 24
 SENT = 8
 UNROLL = 16
-LOAD_ORDER = (8, 9, 10, 7, 6, 0, 1, 5, 3, 4, 2)
+LOADS = ((8,), (9,), (10,), (7,), (6,), (0, 1, 5, 3), (4, 2))
 X_FACE = tuple(row[0] for row in PAIR_INDEX)
 Y_FACE = tuple(row[1] for row in PAIR_INDEX)
 MESH = pl.DeviceIdType.MESH
@@ -133,6 +133,7 @@
     cells_a,
     moments,
     wide,
+    zeros,
     face_send,
     face_recv,
     stress_send,
@@ -141,17 +142,14 @@
     in_ref,
     back_send,
     back_recv,
-    out_s,
+    sent_s,
     out_r,
-    face_s,
     face_r,
-    stress_s,
     stress_r,
-    back_s,
     back_r,
     ) = refs[25:]
     loads = [
-        pltpu.make_async_copy(source, kept, load_s.at[i])
+        pltpu.make_async_copy(source, kept, load_s.at[[i in batch for batch in LOADS].index(True)])
         for i, (source, kept) in enumerate(zip(sources, held))
     ]
     X, Y, Z = spans
@@ -170,8 +168,13 @@
     turns = [j + odd * (n - 2 - 2 * j) for j in range(n - 1)]
     others = [j + lax.div(j + n - me, n) for j in turns]
     group = received // 2
-    base_a = n // 2 * jnp.minimum(lax.div(me, n // 4), 1)
-    base_b = n // 2 - base_a
+    half_a = jnp.minimum(lax.div(me, n // 4), 1)
+    half_b = 1 - half_a
+    base_a, base_b = half_a * (n // 2), half_b * (n // 2)
+    for batch in LOADS:
+        for i in batch:
+            loads[i].start()
+
     barrier = pltpu.get_barrier_semaphore()
     for peer in far + near:
         pl.semaphore_signal(barrier, inc=1, device_id={"yz": peer}, device_id_type=MESH)
@@ -183,9 +186,6 @@
     @pl.when(gx < n_gx - 1)
     def _():
         pl.semaphore_signal(barrier, inc=1, device_id={"gx": gx + 1}, device_id_type=MESH)
-
-    for i in LOAD_ORDER:
-        loads[i].start()
 
     sides = (
         (0, 1, gx > 0, gx == 0, {"gx": gx - 1}),
@@ -193,53 +193,41 @@
         (2, 3, me > 0, me == 0, {"yz": me - 1}),
         (3, 2, me < n - 1, me == n - 1, {"yz": me + 1}),
     )
-    for side, _, _, edge, _ in sides:
-
-        @pl.when(edge)
-        def _(side=side):
-            face_recv[side] = jnp.zeros(face_recv.shape[1:], F32)
-            stress_recv[side] = jnp.zeros(stress_recv.shape[1:], F32)
-
     def face_copy(side, other, where, send, recv, send_sem, recv_sem):
         return pltpu.make_async_remote_copy(
             src_ref=send.at[side],
             dst_ref=recv.at[other],
-            send_sem=send_sem.at[side],
-            recv_sem=recv_sem.at[other],
+            send_sem=send_sem.at[1],
+            recv_sem=recv_sem.at[0],
             device_id=where,
             device_id_type=MESH,
         )
 
     def faces_start(send, recv, send_sem, recv_sem):
-        for side, other, there, _, where in sides:
+        for side, other, there, edge, where in sides:
 
             @pl.when(there)
             def _(side=side, other=other, where=where):
                 face_copy(side, other, where, send, recv, send_sem, recv_sem).start()
 
+            @pl.when(edge)
+            def _(side=side):
+                pltpu.make_async_copy(
+                    zeros.at[pl.ds(0, recv.shape[1])], recv.at[side], recv_sem.at[0]
+                ).start()
+
     def faces_wait(send, recv, send_sem, recv_sem):
-        for side, _, there, _, where in sides:
-
-            @pl.when(there)
-            def _(side=side, where=where):
-                face_copy(side, side, where, send, recv, send_sem, recv_sem).wait_recv()
-
-    def faces_sent(send, recv, send_sem, recv_sem):
-        for side, other, there, _, where in sides:
-
-            @pl.when(there)
-            def _(side=side, other=other, where=where):
-                face_copy(side, other, where, send, recv, send_sem, recv_sem).wait_send()
-
-    face_args = (face_send, face_recv, face_s, face_r)
-    stress_args = (stress_send, stress_recv, stress_s, stress_r)
-
-    def all_copy(peer, source, send, recv, height, pitch, send_sem, recv_sem):
+        arrived(math.prod(recv.shape[:-1]), v_ref, recv_sem.at[0])
+
+    face_args = (face_send, face_recv, sent_s, face_r)
+    stress_args = (stress_send, stress_recv, sent_s, stress_r)
+
+    def all_copy(peer, source, send, recv, height, pitch, parts, send_sem, recv_sem):
         return pltpu.make_async_remote_copy(
             src_ref=send.at[pl.ds(pl.multiple_of(peer * pitch, 8), height), :],
             dst_ref=recv.at[pl.ds(pl.multiple_of(source * pitch, 8), height), :],
-            send_sem=send_sem.at[peer],
-            recv_sem=recv_sem.at[source],
+            send_sem=send_sem.at[0],
+            recv_sem=recv_sem.at[lax.div(source * parts, n)],
             device_id={"yz": peer},
             device_id_type=MESH,
         )
@@ -248,28 +236,27 @@
         for peer in peers:
             all_copy(peer, me, *args).start()
 
-    def all_wait(peers, *args):
-        for peer in peers:
-            all_copy(peer, peer, *args).wait_recv()
-
-    def half_wait(base, *args):
-        for j in range(n // 2):
-            @pl.when(base + j != me)
-            def _(j=j):
-                all_copy(base + j, base + j, *args).wait_recv()
-
-    def all_sent(peers, *args):
-        for peer in peers:
-            all_copy(peer, me, *args).wait_send()
-
-    pay_args = (out_ref, in_ref, SENT * cap + 1, rows, out_s, out_r)
-    back_args = (back_send, back_recv, 3 * cap, back_rows, back_s, back_r)
-
-    def landed(*which):
-        for i in which:
-            loads[i].wait()
-
-    landed(8, 9, 10, 7, 6)
+    def own_copy(send, recv, height, pitch, parts, send_sem, recv_sem):
+        own = pl.ds(pl.multiple_of(me * pitch, 8), height)
+        return pltpu.make_async_copy(send.at[own, :], recv.at[own, :], recv_sem.at[lax.div(me * parts, n)])
+
+    def all_wait(part, send, recv, height, pitch, parts, send_sem, recv_sem):
+        arrived(n // parts * height, v_ref, recv_sem.at[part])
+
+    pay_args = (out_ref, in_ref, SENT * cap + 1, rows, 2, sent_s, out_r)
+    back_args = (back_send, back_recv, 3 * cap, back_rows, 1, sent_s, back_r)
+
+    def arrived(count, buffer, sem):
+        rows = buffer.at[pl.ds(0, count), :]
+        pltpu.make_async_copy(rows, rows, sem).wait()
+
+    def landed(batch):
+        arrived(sum(math.prod(held[i].shape[:-1]) for i in LOADS[batch]), v_ref, load_s.at[batch])
+
+    zeros[...] = jnp.zeros(zeros.shape, F32)
+
+    for batch in range(5):
+        loads[LOADS[batch][0]].wait()
     iota = functools.partial(lax.broadcasted_iota, jnp.int32)
 
     def folded(shape, axis, period):
@@ -296,7 +283,7 @@
     home_t = twice(home_t[:pencils].astype(BF16), 1)
     live = onehot(iota((slots, blocks), 0) < tally[...]).T
 
-    landed(0, 1)
+    landed(5)
     u = [pick(home_hot, flow[c]) for c in range(3)]
     temp = pick(home_hot, heat[...])
     for c in range(4):
@@ -306,7 +293,6 @@
         face_send[2, c] = grid[pl.ds(0, X, stride=Y), :]
         face_send[3, c] = grid[pl.ds(Y - 1, X, stride=Y), :]
 
-    landed(5, 3)
     where = cells[...]
     u = [lanes(u[c], where) for c in range(3)]
     spread = jnp.sqrt((1.0 - DECAY * DECAY) * lanes(temp, where))
@@ -324,17 +310,17 @@
         pencil_row = jnp.where(place == j, pencil_out[j * n : (j + 1) * n], pencil_row)
     out_ref[pl.ds(SENT * cap, n, stride=rows), :] = pencil_row
 
-    landed(4)
+    landed(6)
     for c in range(3):
         send_row(3 + c, pick(from_twice, noise[3 + c]))
 
-    landed(2)
     first = [drift(speed[c], u[c], spread, noise[c]) for c in range(3)]
     for c in range(3):
         send_row(c, pick(from_twice, first[c]))
 
-    expected = n - 1 + jnp.where(gx > 0, 1, 0) + jnp.where(gx < n_gx - 1, 1, 0)
-    pl.semaphore_wait(barrier, expected)
+    near_gx = jnp.where(gx > 0, 1, 0) + jnp.where(gx < n_gx - 1, 1, 0)
+    neighbours = near_gx + jnp.where(me > 0, 1, 0) + jnp.where(me < n - 1, 1, 0)
+    pl.semaphore_wait(barrier, n - 1 + near_gx)
     late = lax.rem(gx, 2) == 1
 
     @pl.when(jnp.logical_not(late))
@@ -342,8 +328,7 @@
         all_start(far + near, *pay_args)
 
     faces_start(*face_args)
-    own = pl.ds(pl.multiple_of(me * rows, 8), rows)
-    in_ref[own, :] = out_ref[own, :]
+    own_copy(*pay_args).start()
 
     second = [drift(first[c], u[c], spread, noise[3 + c]) for c in range(3)]
     for c in range(3):
@@ -371,26 +356,34 @@
             [lanes(pencil_row, jnp.full((n // 2, slots), j * (slots // cap), jnp.int32)) for j in range(cap)], axis=0
         ).astype(jnp.int32)
         hot = onehot(pencil[:, : 2 * pencils] == folded((group, 2 * pencils), 1, pencils))
-        hot_t = twice(hot[:, :pencils], 0).T.astype(BF16)
+        narrow = hot[:, :pencils]
         hot = hot.astype(BF16)
         u = [lanes(pick(hot, flow[c]), where) for c in range(3)]
         spread = jnp.sqrt((1.0 - DECAY * DECAY) * lanes(pick(hot, heat[...]), where))
         second = [drift(got[c], u[c], spread, got[3 + c]) for c in range(3)]
-        put_terms(v_ref, group, got[6], second)
-        deposit(group, v_ref, cells_a.at[side], pb_ref)
-        return where, hot, hot_t, second
-
-    def total(hot_t, k):
-        moments[k] = moments[k] + pick(hot_t, deposited(pb_ref, group, k))
-
-    half_wait(base_a, *pay_args)
-    where_n, hot_n, hot_t, second_n = migrants(0, base_a)
-    for k in range(MOMENTS):
-        total(hot_t, k)
-    half_wait(base_b, *pay_args)
-    where_f, hot_f, hot_t, second_f = migrants(1, base_b)
+        put_terms(v_ref.at[pl.ds(side * group * PITCH, group * PITCH), :], group, got[6], second)
+        deposit(
+            group,
+            v_ref.at[pl.ds(side * group * PITCH, group * PITCH), :],
+            cells_a.at[side],
+            pb_ref.at[pl.ds(side * group // 2 * PITCH, group // 2 * PITCH), :],
+        )
+        return where, hot, narrow, second
+
+    all_wait(half_a, *pay_args)
+    where_n, hot_n, narrow_n, second_n = migrants(0, base_a)
+    all_wait(half_b, *pay_args)
+    where_f, hot_f, narrow_f, second_f = migrants(1, base_b)
+    hot_t = twice(jnp.concatenate([narrow_n, narrow_f], axis=0), 0).T.astype(BF16)
+
+    def total(k):
+        parts = [
+            deposited(pb_ref.at[pl.ds(side * group // 2 * PITCH, group // 2 * PITCH), :], group, k) for side in range(2)
+        ]
+        moments[k] = moments[k] + pick(hot_t, jnp.concatenate(parts, axis=0))
+
     for k in range(4, MOMENTS):
-        total(hot_t, k)
+        total(k)
     for row in range(3):
         k = 4 + X_FACE[row]
         stress_send[0, row] = moments[k, pl.ds(0, Y), :]
@@ -400,7 +393,7 @@
         stress_send[3, row] = moments[k, pl.ds(Y - 1, X, stride=Y), :]
     faces_start(*stress_args)
     for k in range(4):
-        total(hot_t, k)
+        total(k)
 
     lane = iota((pencils, Z), 1)
 
@@ -476,23 +469,24 @@
                     j * (n // 2) : (j + 1) * (n // 2)
                 ]
     all_start(others, *back_args)
-    own = pl.ds(pl.multiple_of(me * back_rows, 8), back_rows)
-    back_recv[own, :] = back_send[own, :]
+    own_copy(*back_args).start()
     for c in range(3):
         w = lanes(dot(home_hot, fresh[c]), where)
         now = second_ref[c]
         second_ref[c] = live * (now + RELAXATION * (w - now))
-    all_wait(others, *back_args)
+    all_wait(0, *back_args)
     for c in range(3):
         returned = jnp.concatenate(
             [back_recv[pl.ds(c * cap + j, n, stride=back_rows), :] for j in range(cap)], axis=0
         )
         speed_out[c] = jnp.where(moved, live * pick(to_block, returned), second_ref[c])
 
-    all_sent(far + near, *pay_args)
-    faces_sent(*face_args)
-    faces_sent(*stress_args)
-    all_sent(others, *back_args)
+    arrived((n - 1) * (pay_args[2] + back_args[2]), v_ref, sent_s.at[0])
+    for count in range(1, 5):
+
+        @pl.when(neighbours == count)
+        def _(count=count):
+            arrived(count * sum(math.prod(x.shape[1:-1]) for x in (face_send, stress_send)), v_ref, sent_s.at[1])
 
 
 def put_out(fields, velocity, fields_out, velocity_out, sems):
@@ -551,7 +545,7 @@
         in_specs=[pl.BlockSpec(memory_space=pltpu.HBM)] * 11,
         out_specs=(vmem, vmem),
         scratch_shapes=[pltpu.VMEM(x.shape, x.dtype) for x in operands]
-        + [pltpu.SemaphoreType.DMA((11,))]
+        + [pltpu.SemaphoreType.DMA((len(LOADS),))]
         + [
             pltpu.VMEM((max(blocks, received) * PITCH, slots), F32),
             pltpu.VMEM((max(blocks, received) // 2 * PITCH, Z), F32),
@@ -559,6 +553,7 @@
             pltpu.VMEM((2, received // 2, slots), jnp.int32),
             pltpu.VMEM((MOMENTS, X * Y, Z), F32),
             pltpu.VMEM((9, X + 2, 24, Z), F32),
+            pltpu.VMEM((4, 8, Z), F32),
             pltpu.VMEM((4, 4, 8, Z), F32),
             pltpu.VMEM((4, 4, 8, Z), F32),
             pltpu.VMEM((4, 3, 8, Z), F32),
@@ -567,14 +562,11 @@
             pltpu.VMEM((n * rows, slots), F32),
             pltpu.VMEM((n * back_rows, slots), F32),
             pltpu.VMEM((n * back_rows, slots), F32),
-            pltpu.SemaphoreType.DMA((n,)),
-            pltpu.SemaphoreType.DMA((n,)),
-            pltpu.SemaphoreType.DMA((4,)),
-            pltpu.SemaphoreType.DMA((4,)),
-            pltpu.SemaphoreType.DMA((4,)),
-            pltpu.SemaphoreType.DMA((4,)),
-            pltpu.SemaphoreType.DMA((n,)),
-            pltpu.SemaphoreType.DMA((n,)),
+            pltpu.SemaphoreType.DMA((2,)),
+            pltpu.SemaphoreType.DMA((2,)),
+            pltpu.SemaphoreType.DMA((1,)),
+            pltpu.SemaphoreType.DMA((1,)),
+            pltpu.SemaphoreType.DMA((1,)),
         ],
         compiler_params=pltpu.CompilerParams(
             collective_id=0, has_side_effects=True, vmem_limit_bytes=32 * 1024 * 1024

time: 20.2 us -> 19.8 us (0.980)
  Pallas kernels: 19.4 us -> 19 us
    pallas_call x1, Pallas kernels: 18.7 us -> 18.2 us  [shards(): pl.pallas_call(functools.partial(kernel, n, n_gx, (X, Y, Z)), out_shape=(...]
where the time goes in v3:
time: 19.8 us; the launch traced here: 19.6 us
  Pallas kernels  19 us (96%)
  between operations  0.64 us (3%)
    pallas_call x1, Pallas kernels, shards(): pl.pallas_call(functools.partial(kernel, n, n_gx, (X, Y, Z)), out_shape=(...  18.2 us
    pallas_call x1, Pallas kernels, shards(): pl.pallas_call(put_out, out_shape=(jax.ShapeDtypeStruct((4, X * Y, Z), F3...  0.74 us

profile of v3, /device:TPU:0, one launch (start us, length us, event | category | flops | bytes accessed | tf_op | source)
XLA Modules:
  0.0 19.6 jit_solution(7194446331262793391)
XLA Ops:
  0.6 18.2 %shard_map.122 = (f32[4,64,128]{2,1,0:T(8,128)S(1)}, f32[3,128,128]{2,1,0:T(8,128)S(1)}) custom-call(f32[3,64,128]{2,1,0:T(8,128)} %bitcast.10, f32[64,128]{1,0:T(8,128)} %bitcast.11, f32[3,128,128]{2,1,0:T(8,128)} %refs_2_.1, f32[128,128]{1,0:T(8,128)} %refs_3_.1, f32[6,128,128]{2,1,0:T(8,128)} %bitcast.9, s32[128,128]{1,0:T(8,128)} %refs_5_.1, ...), custom_call_target="tpu_custom_call" | custom-call | tf_op jit(solution)/shard_map/pallas_call | solution.py:539
  18.9 0.7 %shard_map.123 = (f32[4,64,128]{2,1,0:T(8,128)}, f32[3,128,128]{2,1,0:T(8,128)}) custom-call(f32[4,64,128]{2,1,0:T(8,128)S(1)} %get-tuple-element.6.fields, f32[3,128,128]{2,1,0:T(8,128)S(1)} %get-tuple-element.7.velocity), custom_call_target="tpu_custom_call" | custom-call | tf_op jit(solution)/shard_map/pallas_call | solution.py:576

commit v4 on v3

--- a/solution.py
+++ b/solution.py
@@ -17,6 +17,7 @@
 PAIR_INDEX = ((0, 1, 2), (1, 3, 4), (2, 4, 5))
 MOMENTS = 10
 PITCH = 24
+PAIR_PITCH = 56
 SENT = 8
 UNROLL = 16
 LOADS = ((8,), (9,), (10,), (7,), (6,), (0, 1, 5, 3), (4, 2))
@@ -69,7 +70,7 @@
     return u + DECAY * (start - u) + spread * noise
 
 
-def deposit(count, v_ref, cells_ref, pb_ref, first=0, last=None):
+def deposit(count, v_ref, cells_ref, pb_ref):
     width = v_ref.shape[1]
     slots = cells_ref.shape[1]
     half = count // 2
@@ -81,7 +82,7 @@
     def some(step, carry):
         for t in range(unroll):
             n = step * unroll + t
-            start = pl.multiple_of(n * 2 * PITCH, 2 * PITCH)
+            start = pl.multiple_of(n * PAIR_PITCH, 8)
             rows = [v_ref[pl.ds(start + 8 * part, 8), :] for part in range(6)]
             left = [rows[0], jnp.where(mine, rows[1], 0.0), none, rows[3], jnp.where(mine, rows[4], 0.0), none]
             right = [none, jnp.where(mine, 0.0, rows[1]), rows[2], none, jnp.where(mine, 0.0, rows[4]), rows[5]]
@@ -95,7 +96,7 @@
             pb_ref[pl.ds(pl.multiple_of(n * PITCH, 8), PITCH), :] = out[:PITCH] + out[PITCH:]
         return carry
 
-    lax.fori_loop(first, half // unroll if last is None else last, some, 0)
+    lax.fori_loop(0, half // unroll, some, 0)
 
 
 def put_terms(v_ref, count, weight, second):
@@ -106,7 +107,7 @@
         high = term.astype(BF16).astype(F32)
         for part, value in enumerate((high, term - high)):
             for block in range(2):
-                v_ref[pl.ds(part * PITCH + block * MOMENTS + k, half, stride=2 * PITCH), :] = value[
+                v_ref[pl.ds(part * PITCH + block * MOMENTS + k, half, stride=PAIR_PITCH), :] = value[
                     block * half : (block + 1) * half
                 ]
 
@@ -334,13 +335,11 @@
     for c in range(3):
         second_ref[c] = second[c]
     put_terms(v_ref, blocks, jnp.where(moved, 0.0, weight), second)
-    deposit(blocks, v_ref, cells, pb_ref, 0, 3)
+    deposit(blocks, v_ref, cells, pb_ref)
 
     @pl.when(late)
     def _():
         all_start(far + near, *pay_args)
-
-    deposit(blocks, v_ref, cells, pb_ref, 3)
     for k in range(MOMENTS):
         moments[k] = pick(home_t, deposited(pb_ref, blocks, k))
 
@@ -361,10 +360,10 @@
         u = [lanes(pick(hot, flow[c]), where) for c in range(3)]
         spread = jnp.sqrt((1.0 - DECAY * DECAY) * lanes(pick(hot, heat[...]), where))
         second = [drift(got[c], u[c], spread, got[3 + c]) for c in range(3)]
-        put_terms(v_ref.at[pl.ds(side * group * PITCH, group * PITCH), :], group, got[6], second)
+        put_terms(v_ref.at[pl.ds(side * group // 2 * PAIR_PITCH, group // 2 * PAIR_PITCH), :], group, got[6], second)
         deposit(
             group,
-            v_ref.at[pl.ds(side * group * PITCH, group * PITCH), :],
+            v_ref.at[pl.ds(side * group // 2 * PAIR_PITCH, group // 2 * PAIR_PITCH), :],
             cells_a.at[side],
             pb_ref.at[pl.ds(side * group // 2 * PITCH, group // 2 * PITCH), :],
         )
@@ -521,7 +520,7 @@
     cap = 2 * moving // n
     received = n * cap
     rows = -(-(SENT * cap + 1) // 8) * 8
-    back_rows = -(-3 * cap // 8) * 8
+    back_rows = -(-3 * cap // 8) * 8 + 8
     operands = (
         flow_speed_field.reshape(3, X * Y, Z),
         thermal_field.reshape(X * Y, Z),
@@ -547,7 +546,7 @@
         scratch_shapes=[pltpu.VMEM(x.shape, x.dtype) for x in operands]
         + [pltpu.SemaphoreType.DMA((len(LOADS),))]
         + [
-            pltpu.VMEM((max(blocks, received) * PITCH, slots), F32),
+            pltpu.VMEM((max(blocks, received) // 2 * PAIR_PITCH, slots), F32),
             pltpu.VMEM((max(blocks, received) // 2 * PITCH, Z), F32),
             pltpu.VMEM((3, blocks, slots), F32),
             pltpu.VMEM((2, received // 2, slots), jnp.int32),

time: 19.8 us -> 19.7 us (level)
  no operation moved by 1% of the time
where the time goes in v4:
time: 19.7 us; the launch traced here: 19.5 us
  Pallas kernels  18.9 us (96%)
  between operations  0.64 us (3%)
    pallas_call x1, Pallas kernels, shards(): pl.pallas_call(functools.partial(kernel, n, n_gx, (X, Y, Z)), out_shape=(...  18.2 us
    pallas_call x1, Pallas kernels, shards(): pl.pallas_call(put_out, out_shape=(jax.ShapeDtypeStruct((4, X * Y, Z), F3...  0.74 us

profile of v4, /device:TPU:0, one launch (start us, length us, event | category | flops | bytes accessed | tf_op | source)
XLA Modules:
  0.0 19.5 jit_solution(12976451545010431191)
XLA Ops:
  0.6 18.2 %shard_map.122 = (f32[4,64,128]{2,1,0:T(8,128)S(1)}, f32[3,128,128]{2,1,0:T(8,128)S(1)}) custom-call(f32[3,64,128]{2,1,0:T(8,128)} %bitcast.10, f32[64,128]{1,0:T(8,128)} %bitcast.11, f32[3,128,128]{2,1,0:T(8,128)} %refs_2_.1, f32[128,128]{1,0:T(8,128)} %refs_3_.1, f32[6,128,128]{2,1,0:T(8,128)} %bitcast.9, s32[128,128]{1,0:T(8,128)} %refs_5_.1, ...), custom_call_target="tpu_custom_call" | custom-call | tf_op jit(solution)/shard_map/pallas_call | solution.py:538
  18.8 0.7 %shard_map.123 = (f32[4,64,128]{2,1,0:T(8,128)}, f32[3,128,128]{2,1,0:T(8,128)}) custom-call(f32[4,64,128]{2,1,0:T(8,128)S(1)} %get-tuple-element.6.fields, f32[3,128,128]{2,1,0:T(8,128)S(1)} %get-tuple-element.7.velocity), custom_call_target="tpu_custom_call" | custom-call | tf_op jit(solution)/shard_map/pallas_call | solution.py:575

commit v5 on v4

--- a/solution.py
+++ b/solution.py
@@ -125,7 +125,8 @@
     spans,
     *refs,
 ):
-    sources, (fields_out, speed_out), held, load_s = refs[:11], refs[11:13], refs[13:24], refs[24]
+    sources, results, held, load_s = refs[:11], refs[11:16], refs[16:27], refs[27]
+    fields_out, speed_out, returned_out, to_block_out, live_out = results
     flow, heat, speed, mass, noise, cells, tally, home, table, target, entered = held
     (
     v_ref,
@@ -148,7 +149,7 @@
     face_r,
     stress_r,
     back_r,
-    ) = refs[25:]
+    ) = refs[28:]
     loads = [
         pltpu.make_async_copy(source, kept, load_s.at[[i in batch for batch in LOADS].index(True)])
         for i, (source, kept) in enumerate(zip(sources, held))
@@ -472,13 +473,14 @@
     for c in range(3):
         w = lanes(dot(home_hot, fresh[c]), where)
         now = second_ref[c]
-        second_ref[c] = live * (now + RELAXATION * (w - now))
+        speed_out[c] = jnp.where(moved, 0.0, live * (now + RELAXATION * (w - now)))
+    to_block_out[...] = to_block
+    live_out[...] = live
     all_wait(0, *back_args)
     for c in range(3):
-        returned = jnp.concatenate(
+        returned_out[c] = jnp.concatenate(
             [back_recv[pl.ds(c * cap + j, n, stride=back_rows), :] for j in range(cap)], axis=0
         )
-        speed_out[c] = jnp.where(moved, live * pick(to_block, returned), second_ref[c])
 
     arrived((n - 1) * (pay_args[2] + back_args[2]), v_ref, sent_s.at[0])
     for count in range(1, 5):
@@ -488,13 +490,13 @@
             arrived(count * sum(math.prod(x.shape[1:-1]) for x in (face_send, stress_send)), v_ref, sent_s.at[1])
 
 
-def put_out(fields, velocity, fields_out, velocity_out, sems):
-    copies = (
-        pltpu.make_async_copy(fields, fields_out, sems.at[0]),
-        pltpu.make_async_copy(velocity, velocity_out, sems.at[1]),
-    )
-    for copy in copies:
-        copy.start()
+def put_out(fields, velocity, returned, to_block, live, fields_out, velocity_out, whole, sems):
+    copies = [pltpu.make_async_copy(fields, fields_out, sems.at[3])]
+    copies[0].start()
+    for c in range(3):
+        whole[c] = velocity[c] + live[...] * pick(to_block[...], returned[c])
+        copies.append(pltpu.make_async_copy(whole.at[c], velocity_out.at[c], sems.at[c]))
+        copies[-1].start()
     for copy in copies:
         copy.wait()
 
@@ -535,14 +537,17 @@
         entered_strip_slot.reshape(1, moving),
     )
     vmem = pl.BlockSpec(memory_space=pltpu.VMEM)
-    fields, velocity = pl.pallas_call(
+    parts = pl.pallas_call(
         functools.partial(kernel, n, n_gx, (X, Y, Z)),
         out_shape=(
             pltpu.VMEM((4, X * Y, Z), F32),
             pltpu.VMEM((3, blocks, slots), F32),
+            pltpu.VMEM((3, received, slots), F32),
+            pltpu.VMEM((blocks, 2 * received), BF16),
+            pltpu.VMEM((blocks, slots), F32),
         ),
         in_specs=[pl.BlockSpec(memory_space=pltpu.HBM)] * 11,
-        out_specs=(vmem, vmem),
+        out_specs=(vmem,) * 5,
         scratch_shapes=[pltpu.VMEM(x.shape, x.dtype) for x in operands]
         + [pltpu.SemaphoreType.DMA((len(LOADS),))]
         + [
@@ -578,11 +583,11 @@
             jax.ShapeDtypeStruct((4, X * Y, Z), F32),
             jax.ShapeDtypeStruct((3, blocks, slots), F32),
         ),
-        in_specs=[vmem, vmem],
+        in_specs=[vmem] * 5,
         out_specs=(hbm, hbm),
-        scratch_shapes=[pltpu.SemaphoreType.DMA((2,))],
+        scratch_shapes=[pltpu.VMEM((3, blocks, slots), F32), pltpu.SemaphoreType.DMA((4,))],
         compiler_params=pltpu.CompilerParams(vmem_limit_bytes=32 * 1024 * 1024),
-    )(fields, velocity)
+    )(*parts)
     return fields.reshape(4, X, Y, Z), velocity
 
 

time: 19.7 us -> 19.7 us (level)
  no operation moved by 1% of the time
where the time goes in v5:
time: 19.7 us; the launch traced here: 19.5 us
  Pallas kernels  18.9 us (96%)
  between operations  0.64 us (3%)
    pallas_call x1, Pallas kernels, shards(): pl.pallas_call(functools.partial(kernel, n, n_gx, (X, Y, Z)), out_shape=(...  18 us
    pallas_call x1, Pallas kernels, shards(): pl.pallas_call(put_out, out_shape=(jax.ShapeDtypeStruct((4, X * Y, Z), F3...  0.85 us

profile of v5, /device:TPU:0, one launch (start us, length us, event | category | flops | bytes accessed | tf_op | source)
XLA Modules:
  0.0 19.5 jit_solution(7931749298902262299)
XLA Ops:
  0.6 18.0 %shard_map.122 = (f32[4,64,128]{2,1,0:T(8,128)S(1)}, f32[3,128,128]{2,1,0:T(8,128)S(1)}, f32[3,32,128]{2,1,0:T(8,128)S(1)}, bf16[128,64]{1,0:T(8,128)(2,1)S(1)}, f32[128,128]{1,0:T(8,128)S(1)}) custom-call(f32[3,64,128]{2,1,0:T(8,128)} %bitcast.10, f32[64,128]{1,0:T(8,128)} %bitcast.11, f32[3,128,128]{2,1,0:T(8,128)} %refs_2_.1, f32[128,128]{1,0:T(8,128)} %refs_3_.1, ...), custom_call_target="tpu_custom_call" | custom-call | tf_op jit(solution)/shard_map/pallas_call | solution.py:540
  18.7 0.8 %shard_map.123 = (f32[4,64,128]{2,1,0:T(8,128)}, f32[3,128,128]{2,1,0:T(8,128)}) custom-call(f32[4,64,128]{2,1,0:T(8,128)S(1)} %get-tuple-element.9.fields, f32[3,128,128]{2,1,0:T(8,128)S(1)} %get-tuple-element.10.velocity, f32[3,32,128]{2,1,0:T(8,128)S(1)} %get-tuple-element.11.returned, bf16[128,64]{1,0:T(8,128)(2,1)S(1)} %get-tuple-element.12.to_block, ...), custom_call_target="tpu_custom_call" | custom-call | tf_op jit(solution)/shard_map/pallas_call | solution.py:580
